TPU v7x, 256 devices: a whole 4x4x8 slice. The times are simulated.
256 devices in a mesh: chan: 16 (over y, x), filt: 8 (over z), space: 2 (over core).
Axes of the slice: x: 4, y: 4, z: 8, core: 2. Of those that a mesh axis runs over, the one named last changes fastest.
Arguments:
- voxels: bfloat16 [128, 512, 256], P(('space', 'filt'), 'chan'), may hold values from -6 to 6
- filters: bfloat16 [27, 512, 512], P(None, 'chan', 'filt'), may hold values from -0.0546875 to 0.0546875
- upstream: bfloat16 [128, 512, 256], P(('space', 'chan'), 'filt'), may hold values from -6 to 6
Outputs:
- responses: bfloat16 [128, 512, 256], P(('space', 'chan'), 'filt')
- voxel_grad: bfloat16 [128, 512, 256], P(('space', 'filt'), 'chan')
- filter_grad: float32 [27, 512, 512], P(None, 'chan', 'filt')
All inputs are finite; a program needn't handle non-finite values.
Results may differ from a plain program's by a relative error of at most 0.001.
Values may be sent and summed in bfloat16 or wider, within the bound.
A program may use at most 64 MiB of HBM per device.

v0:
```python
import math

import jax
import jax.numpy as jnp
from jax import lax
from jax.sharding import PartitionSpec as P

PLANE_Z = 16


plane_offsets = [(step_y, step_z) for step_y in (-1, 0, 1) for step_z in (-1, 0, 1)]


def padded_2(block, sides, width):
    for axis, dim in sides:
        count = lax.axis_size(axis)
        forward = [(i, i + 1) for i in range(count - 1)]
        backward = [(target, source) for source, target in forward]
        low = lax.ppermute(
            lax.slice_in_dim(block, block.shape[dim] - width, None, axis=dim), axis, forward
        )
        high = lax.ppermute(lax.slice_in_dim(block, 0, width, axis=dim), axis, backward)
        block = jnp.concatenate([low, block, high], axis=dim)
    return block


def plane_shift(segment, step_y, step_z):
    plane_len = segment.shape[-1]
    pad_width = PLANE_Z + 1
    padded = jnp.pad(segment, ((0, 0), (0, 0), (pad_width, pad_width)))
    offset = step_y * PLANE_Z + step_z
    shifted_block = lax.slice_in_dim(
        padded, pad_width + offset, pad_width + offset + plane_len, axis=2
    )
    column = jnp.arange(plane_len) % PLANE_Z + step_z
    inside = (column >= 0) & (column < PLANE_Z)
    return jnp.where(inside, shifted_block, jnp.zeros_like(shifted_block))


def conv_rows(padded, kernel, facing, row_count, tap_group):
    in_width = kernel.shape[2]
    out_width = kernel.shape[3]
    plane_len = padded.shape[2]
    slab_rows = math.gcd(row_count, 4)
    loop_turns = row_count // slab_rows

    def slab_term(position):
        segment = lax.dynamic_slice_in_dim(padded, position * slab_rows, slab_rows + 2, 0)
        running = jnp.zeros((slab_rows, out_width, plane_len), jnp.float32)
        shifted = [
            plane_shift(segment, facing * step_y, facing * step_z)
            for step_y, step_z in plane_offsets[0:tap_group]
        ]
        stacked = jnp.concatenate(shifted, axis=1)
        for offset_x in range(3):
            tap_kernel = kernel[offset_x, 0:tap_group].reshape(tap_group * in_width, out_width)
            running = running + jnp.einsum(
                "rkv,kf->rfv",
                stacked[offset_x : offset_x + slab_rows],
                tap_kernel,
                preferred_element_type=jnp.float32,
            )
        return running

    pieces = lax.map(slab_term, jnp.arange(loop_turns, dtype=jnp.int32))
    return pieces.reshape(row_count, out_width, plane_len)


def local(voxels, filters, upstream):
    local_c = filters.shape[1]
    local_f = filters.shape[2]
    plane_len = voxels.shape[2]
    gathered = lax.all_gather(voxels, "filt", axis=0, tiled=True)
    all_rows = gathered.shape[0]
    margin = padded_2(gathered, (("space", 0),), 1)
    kernel = filters.reshape(3, 9, local_c, local_f)
    own_rows = all_rows // lax.axis_size("chan")
    responses = lax.psum_scatter(
        conv_rows(margin, kernel, 1, own_rows * lax.axis_size("chan"), 9),
        "chan",
        scatter_dimension=0,
        tiled=True,
    ).astype(jnp.bfloat16)
    upstream_rows = lax.all_gather(upstream, "chan", axis=0, tiled=True)
    upstream_margin = padded_2(upstream_rows, (("space", 0),), 1)
    flipped = kernel[::-1].transpose(0, 1, 3, 2)
    voxel_grad = lax.psum_scatter(
        conv_rows(
            upstream_margin,
            flipped,
            -1,
            all_rows // lax.axis_size("filt") * lax.axis_size("filt"),
            9,
        ),
        "filt",
        scatter_dimension=0,
        tiled=True,
    ).astype(jnp.bfloat16)
    slab_rows = math.gcd(all_rows, 4)
    loop_turns = all_rows // slab_rows

    def accumulate(position, running):
        segment = lax.dynamic_slice_in_dim(margin, position * slab_rows, slab_rows + 2, 0)
        stacked = jnp.concatenate(
            [plane_shift(segment, step_y, step_z) for step_y, step_z in plane_offsets], axis=1
        )
        cotangent = lax.dynamic_slice_in_dim(upstream_rows, position * slab_rows, slab_rows, 0)
        products = [
            jnp.einsum(
                "rkv,rfv->kf",
                stacked[offset_x : offset_x + slab_rows],
                cotangent,
                preferred_element_type=jnp.float32,
            )
            for offset_x in range(3)
        ]
        return running + jnp.stack(products)

    running = lax.fori_loop(
        0, loop_turns, accumulate, jnp.zeros((3, 9 * local_c, local_f), jnp.float32)
    )
    summed = lax.psum(running, "space")
    scaling = jnp.sqrt(jnp.float32(all_rows * lax.axis_size("space") * plane_len))
    filter_grad = summed.reshape(27, local_c, local_f) / scaling
    return (responses, voxel_grad, filter_grad)


def solution(mesh):
    return jax.shard_map(
        local,
        mesh=mesh,
        in_specs=(
            P(("space", "filt"), "chan", None),
            P(None, "chan", "filt"),
            P(("space", "chan"), "filt", None),
        ),
        out_specs=(
            P(("space", "chan"), "filt", None),
            P(("space", "filt"), "chan", None),
            P(None, "chan", "filt"),
        ),
        check_vma=False,
    )
```

profile of v0, /device:TPU:32, one launch (start us, length us, event | category | flops | bytes accessed | tf_op | source)
XLA Modules:
  0.0 468.7 jit_solution(6133946709356821817)
XLA Ops:
  8.7 41.5 %all-gather.3.cloned.1.call-done = bf16[64,32,256]{2,1,0:T(8,128)(2,1)} async-done(((bf16[8,32,256]{2,1,0:T(8,128)(2,1)}), bf16[64,32,256]{2,1,0:T(8,128)(2,1)}) %all-gather.3.cloned.1.call-update) | async-done | bytes 1048592 | tf_op jit(solution)/shard_map/all_gather | solution.py:73
  51.0 1.3 collective-permute-start
  53.4 1.3 collective-permute-start.1
  54.8 1.7 collective-permute-done.1
  56.5 45.1 %all-gather.5.cloned.1.call-done = bf16[64,64,256]{2,1,0:T(8,128)(2,1)} async-done(((bf16[4,64,256]{2,1,0:T(8,128)(2,1)}), bf16[64,64,256]{2,1,0:T(8,128)(2,1)}) %all-gather.5.cloned.1.call-update) | async-done | bytes 2097168 | tf_op jit(solution)/shard_map/all_gather | solution.py:84
  102.3 1.3 collective-permute-start.2
  103.6 1.3 collective-permute-start.3
  104.9 77.3 %while.42 = (s32[]{:T(128)}, f32[3,288,64]{1,2,0:T(8,128)S(1)}, bf16[66,32,256]{2,1,0:T(8,128)(2,1)S(1)}, bf16[64,64,256]{2,1,0:T(8,128)(2,1)}, s32[]{:T(128)}, ...) while((s32[]{:T(128)}, f32[3,288,64]{1,2,0:T(8,128)S(1)}, bf16[66,32,256]{2,1,0:T(8,128)(2,1)S(1)}, ...), condition=%wide.region_7.8_spmd.clone, body=%wide.region_6.7_spmd.clone.sunk | while | flops 113917192 | bytes 5903554 | solution.py:119
  105.9 1.2 convolution_bitcast_fusion.7
  107.1 1.2 convolution_bitcast_fusion.8
  108.4 1.2 convolution_bitcast_fusion.6
  110.7 1.2 convolution_bitcast_fusion.7
  112.0 1.2 convolution_bitcast_fusion.8
  113.2 1.2 convolution_bitcast_fusion.6
  116.8 1.2 convolution_bitcast_fusion.8
  118.1 1.2 convolution_bitcast_fusion.6
  121.6 1.2 convolution_bitcast_fusion.8
  122.9 1.2 convolution_bitcast_fusion.6
  126.5 1.2 convolution_bitcast_fusion.8
  127.7 1.2 convolution_bitcast_fusion.6
  131.3 1.2 convolution_bitcast_fusion.8
  132.5 1.2 convolution_bitcast_fusion.6
  136.1 1.2 convolution_bitcast_fusion.8
  137.4 1.2 convolution_bitcast_fusion.6
  140.9 1.2 convolution_bitcast_fusion.8
  142.2 1.2 convolution_bitcast_fusion.6
  145.8 1.2 convolution_bitcast_fusion.8
  147.0 1.2 convolution_bitcast_fusion.6
  150.6 1.2 convolution_bitcast_fusion.8
  151.9 1.2 convolution_bitcast_fusion.6
  155.4 1.2 convolution_bitcast_fusion.8
  156.7 1.2 convolution_bitcast_fusion.6
  160.3 1.2 convolution_bitcast_fusion.8
  161.5 1.2 convolution_bitcast_fusion.6
  165.1 1.2 convolution_bitcast_fusion.8
  166.3 1.2 convolution_bitcast_fusion.6
  169.9 1.2 convolution_bitcast_fusion.8
  171.2 1.2 convolution_bitcast_fusion.6
  174.7 1.2 convolution_bitcast_fusion.8
  176.0 1.2 convolution_bitcast_fusion.6
  179.6 1.2 convolution_bitcast_fusion.8
  180.8 1.2 convolution_bitcast_fusion.6
  183.0 3.2 pad_maximum_fusion
  186.3 100.6 %while.41 = (s32[]{:T(128)}, f32[16,4,32,256]{3,2,1,0:T(8,128)}, s32[16]{0:T(128)S(1)}, bf16[66,64,256]{2,1,0:T(8,128)(2,1)}, bf16[3,9,64,32]{2,1,3,0:T(8,128)(2...) while((s32[]{:T(128)}, f32[16,4,32,256]{3,2,1,0:T(8,128)}, s32[16]{0:T(128)S(1)}, ...), condition=%wide.region_4.5_spmd, body=%wide.region_3.4_spmd.sunk | while | flops 114203904 | bytes 8697503 | solution.py:65
  287.8 89.0 %while.40 = (s32[]{:T(128)}, f32[16,4,64,256]{3,2,1,0:T(8,128)}, s32[16]{0:T(128)S(1)}, bf16[66,32,256]{2,1,0:T(8,128)(2,1)}, bf16[3,9,32,64]{3,2,1,0:T(8,128)(2...) while((s32[]{:T(128)}, f32[16,4,64,256]{3,2,1,0:T(8,128)}, s32[16]{0:T(128)S(1)}, ...), condition=%wide.region_1.2_spmd, body=%wide.region_0.1_spmd.sunk | while | flops 113827072 | bytes 6268575 | solution.py:65
  378.8 1.6 convert_element_type.46
  380.4 80.1 %reduce-scatter.3.cloned.1.call-done = f32[4,64,256]{2,1,0:T(8,128)} async-done(((f32[64,64,256]{2,1,0:T(8,128)}), f32[4,64,256]{2,1,0:T(8,128)}) %reduce-scatter.3.cloned.1.call-update) | async-done | bytes 262160 | tf_op jit(solution)/shard_map/reduce_scatter | solution.py:78
  460.5 1.6 convert_element_type.45
  (899 shorter events, 205.7 us)
Async XLA Ops:
  7.2 43.0 %all-gather.3.cloned.1.call-start = ((), (), s32[]{:S(2)}) async-start(), calls=%async_computation.2 | async-start | bytes 1179648 | tf_op jit(solution)/shard_map/all_gather | solution.py:73
  7.9 93.7 %all-gather.5.cloned.1.call-start = ((), (), s32[]{:S(2)}) async-start(), calls=%async_computation.4 | async-start | bytes 2228224 | tf_op jit(solution)/shard_map/all_gather | solution.py:84
  8.6 368.2 %all-reduce.5.cloned.1.call-start = ((), (), s32[]{:S(2)}) async-start(), calls=%async_computation.6 | async-start | bytes 589824 | tf_op jit(solution)/shard_map/psum | solution.py:122
  50.2 4.5 copy-start.3
  51.0 3.7 collective-permute-start
  53.4 3.1 collective-permute-start.1
  102.3 80.7 %collective-permute-start.2 = (bf16[1,64,256]{2,1,0:T(8,128)(2,1)S(1)}, bf16[1,64,256]{2,1,0:T(8,128)(2,1)S(1)}, u32[]{:S(2)}, u32[]{:S(2)}) collective-permute-start(bf16[1,64,256]{2,1,0:T(8,128)(2,1)S(1)} %get-tuple-element.316), channel_id=1, source_target_pairs={{0,1},{2,3},{4,5},{6,7},{8,9},{10,11},{12,13},{14,15},{16,17},{18,... | collective-permute-start | bytes 98312 | tf_op jit(solution)/shard_map/ppermute | solution.py:19
  103.6 79.4 %collective-permute-start.3 = (bf16[1,64,256]{2,1,0:T(8,128)(2,1)S(1)}, bf16[1,64,256]{2,1,0:T(8,128)(2,1)S(1)}, u32[]{:S(2)}, u32[]{:S(2)}) collective-permute-start(bf16[1,64,256]{2,1,0:T(8,128)(2,1)S(1)} %get-tuple-element.317), channel_id=1, source_target_pairs={{1,0},{3,2},{5,4},{7,6},{9,8},{11,10},{13,12},{15,14},{17,16},{19,... | collective-permute-start | bytes 98312 | tf_op jit(solution)/shard_map/ppermute | solution.py:22
  182.2 0.7 copy-start
  182.2 4.0 copy-start.2
  182.9 195.9 %reduce-scatter.5.cloned.1.call-start = ((), (), s32[]{:S(2)}) async-start(), calls=%async_computation.5 | async-start | bytes 2359296 | tf_op jit(solution)/shard_map/reduce_scatter | solution.py:87
  286.9 0.9 copy-start.1
  286.9 173.6 %reduce-scatter.3.cloned.1.call-start = ((), (), s32[]{:S(2)}) async-start(), calls=%async_computation.3 | async-start | bytes 4456448 | tf_op jit(solution)/shard_map/reduce_scatter | solution.py:78
Sparse Core Ops, SparseCore 0:
  9.8 40.3 all-gather.2
  52.6 48.8 all-gather.4
  183.1 29.3 all-reduce.4
  287.0 42.2 reduce-scatter.4
  376.9 83.5 reduce-scatter.2
where the time goes:
time: 472 us; the launch traced here: 469 us
  waiting for transfers between devices  170 us (36%)
  matrix products  111 us (24%)
  other arithmetic  80.9 us (17%)
  local copies, waits for them, and re-layouts  61.4 us (13%)
  loops' own time  26.6 us (6%)
  between operations  13.9 us (3%)
  starting transfers between devices  5.34 us (1%)
    reduce_scatter x1, waiting for transfers between devices, local(): lax.psum_scatter(conv_rows(margin, kernel, 1, own_rows * lax.axis_size('c...  80.1 us
    while x384, other arithmetic  65.8 us
    dot_general x48, matrix products, accumulate(): jnp.einsum('rkv,rfv->kf', stacked[offset_x:offset_x + slab_rows], cotange...  59.9 us
    dot_general x96, matrix products, slab_term(): jnp.einsum('rkv,kf->rfv', stacked[offset_x:offset_x + slab_rows], tap_ker...  50.8 us
    all_gather x1, waiting for transfers between devices, local(): upstream_rows = lax.all_gather(upstream, 'chan', axis=0, tiled=True)  45.1 us
    all_gather x1, waiting for transfers between devices, local(): gathered = lax.all_gather(voxels, 'filt', axis=0, tiled=True)  41.5 us
    dynamic_slice x32, local copies, waits for them, and re-layouts, slab_term(): lax.dynamic_slice_in_dim(padded, position * slab_rows, slab_rows + 2, 0)  29.7 us
    another operation x2, loops' own time, conv_rows(): pieces = lax.map(slab_term, jnp.arange(loop_turns, dtype=jnp.int32))  24.1 us
  transfers between devices with their start and end apart: 9, of which 4 were waited for; matrix products, arithmetic and copies ran while one was open for 53% of the time, Pallas kernels for 0%

commit v1 on v0

v1 whole, which is shorter than its diff:
```python
import jax
import jax.numpy as jnp
from jax import lax
from jax.experimental import pallas as pl
from jax.experimental.pallas import tpu as pltpu
from jax.sharding import PartitionSpec as P

OFFSETS = [(dy, dz) for dy in (-1, 0, 1) for dz in (-1, 0, 1)]
GROUP = 4


def tap_masks():
    lane = lax.broadcasted_iota(jnp.int32, (1, 256), 1)
    z = lane & 15
    y = lane >> 4
    out = []
    for dy, dz in OFFSETS:
        ok = (y + dy >= 0) & (y + dy < 16) & (z + dz >= 0) & (z + dz < 16)
        out.append(jnp.where(ok, 1.0, 0.0).astype(jnp.float32))
    return out


def columns(x, masks, sign):
    parts = []
    for i in range(9):
        dy, dz = OFFSETS[i]
        off = sign * (dy * 16 + dz)
        if off == 0:
            parts.append(x)
            continue
        mask = masks[i if sign > 0 else 8 - i]
        parts.append(pltpu.roll(x, (-off) % 256, 1) * mask.astype(x.dtype))
    return jnp.concatenate(parts, axis=0)


def spread(acc, base, width, ys):
    n = len(ys)
    for i in range(n + 2):
        total = None
        for j in range(max(0, i - 2), min(n, i + 1)):
            part = ys[j][width * (i - j) : width * (i - j + 1), :]
            total = part if total is None else total + part
        rows = pl.ds(pl.multiple_of(base + i * width, width), width)
        acc[rows, :] = acc[rows, :] + total


def conv_kernel(xv, uv, fl, pf, pd, dw, wf, wd, accf, accd, accw):
    for a in range(3):
        w = fl[9 * a : 9 * a + 9].reshape(288, 64)
        wf[64 * (2 - a) : 64 * (3 - a), :] = w.astype(jnp.float32).T.astype(jnp.bfloat16)
        for t in range(9):
            wd[32 * a : 32 * a + 32, 64 * t : 64 * t + 64] = fl[9 * a + t]
    accf[...] = jnp.zeros_like(accf)
    accd[...] = jnp.zeros_like(accd)
    accw[...] = jnp.zeros_like(accw)
    masks = tap_masks()

    def forward(b):
        cols = [columns(xv[b * GROUP + j + 1], masks, 1) for j in range(GROUP)]
        ys = [jnp.dot(wf[...], c, preferred_element_type=jnp.float32) for c in cols]
        spread(accf, (b * GROUP + 1) * 64, 64, ys)
        around = [
            uv[pl.ds(pl.multiple_of((b * GROUP + j) * 64, 64), 192), :] for j in range(GROUP)
        ]
        accw[...] = accw[...] + lax.dot_general(
            jnp.concatenate(cols, axis=1),
            jnp.concatenate(around, axis=1),
            (((1,), (1,)), ((), ())),
            preferred_element_type=jnp.float32,
        )

    def backward(b):
        ys = []
        for j in range(GROUP):
            plane = uv[pl.ds(pl.multiple_of((b * GROUP + j + 1) * 64, 64), 64), :]
            ys.append(
                jnp.dot(wd[...], columns(plane, masks, -1), preferred_element_type=jnp.float32)
            )
        spread(accd, (b * GROUP + 1) * 32, 32, ys)

    for q in (0, 65):
        spread(accf, q * 64, 64, [jnp.dot(wf[...], columns(xv[q], masks, 1), preferred_element_type=jnp.float32)])
        plane = uv[q * 64 : q * 64 + 64, :]
        spread(accd, q * 32, 32, [jnp.dot(wd[...], columns(plane, masks, -1), preferred_element_type=jnp.float32)])

    @pl.loop(0, 64 // GROUP)
    def _(b):
        forward(b)
        backward(b)

    pf[...] = accf[128 : 128 + 4096, :]
    pd[...] = accd[64 : 64 + 2048, :]
    for a in range(3):
        for t in range(9):
            dw[9 * a + t] = accw[32 * t : 32 * t + 32, 64 * (2 - a) : 64 * (3 - a)]


def convolutions(xv, uv, fl):
    return pl.pallas_call(
        conv_kernel,
        out_shape=(
            jax.ShapeDtypeStruct((4096, 256), jnp.float32),
            jax.ShapeDtypeStruct((2048, 256), jnp.float32),
            jax.ShapeDtypeStruct((27, 32, 64), jnp.float32),
        ),
        in_specs=[pl.BlockSpec(memory_space=pltpu.VMEM)] * 3,
        out_specs=[pl.BlockSpec(memory_space=pltpu.VMEM)] * 3,
        scratch_shapes=[
            pltpu.VMEM((192, 288), jnp.bfloat16),
            pltpu.VMEM((96, 576), jnp.bfloat16),
            pltpu.VMEM((68 * 64, 256), jnp.float32),
            pltpu.VMEM((68 * 32, 256), jnp.float32),
            pltpu.VMEM((288, 192), jnp.float32),
        ],
        compiler_params=pltpu.CompilerParams(vmem_limit_bytes=60 * 2**20),
    )(xv, uv, fl)


def with_halo(block):
    low = lax.ppermute(block[-1:], "space", [(0, 1)])
    high = lax.ppermute(block[:1], "space", [(1, 0)])
    return jnp.concatenate([low, block, high], axis=0)


def local(voxels, filters, upstream):
    xv = with_halo(lax.all_gather(voxels, "filt", axis=0, tiled=True))
    uv = with_halo(lax.all_gather(upstream, "chan", axis=0, tiled=True))
    pf, pd, dw = convolutions(xv, uv.reshape(66 * 64, 256), filters)
    responses = lax.psum_scatter(pf.reshape(64, 64, 256), "chan", scatter_dimension=0, tiled=True)
    voxel_grad = lax.psum_scatter(pd.reshape(64, 32, 256), "filt", scatter_dimension=0, tiled=True)
    filter_grad = lax.psum(dw, "space") / jnp.sqrt(jnp.float32(128 * 256))
    return (responses.astype(jnp.bfloat16), voxel_grad.astype(jnp.bfloat16), filter_grad)


def solution(mesh):
    return jax.shard_map(
        local,
        mesh=mesh,
        in_specs=(
            P(("space", "filt"), "chan", None),
            P(None, "chan", "filt"),
            P(("space", "chan"), "filt", None),
        ),
        out_specs=(
            P(("space", "chan"), "filt", None),
            P(("space", "filt"), "chan", None),
            P(None, "chan", "filt"),
        ),
        check_vma=False,
    )
```

time: 472 us -> 298 us (0.63)
  matrix products: 111 us -> 0 us
  waiting for transfers between devices: 170 us -> 249 us
  other arithmetic: 80.9 us -> 9.16 us
  local copies, waits for them, and re-layouts: 61.4 us -> 1.67 us
  loops' own time: 26.6 us -> 0 us
  Pallas kernels: 0 us -> 18.7 us
    dot_general x144 -> x0, matrix products: 111 us -> none  [the longest x48 59.9 us: accumulate(): jnp.einsum('rkv,rfv->kf', stacked[offset_x:offset_x + slab_rows], cotange...]
    while x384 -> x0, other arithmetic: 65.8 us -> none
    reduce_scatter x2, waiting for transfers between devices: 80.1 us -> 129 us  [the longest x1 84.7 us: local(): lax.psum_scatter(pf.reshape(64, 64, 256), 'chan', scatter_dimension=0, ti...]
    dynamic_slice x80 -> x0, local copies, waits for them, and re-layouts: 48.5 us -> none  [the longest x32 29.7 us: slab_term(): lax.dynamic_slice_in_dim(padded, position * slab_rows, slab_rows + 2, 0)]
    psum x1, waiting for transfers between devices: 0.02 us -> 28.5 us  [local(): filter_grad = lax.psum(dw, 'space') / jnp.sqrt(jnp.float32(128 * 256))]
    another operation x3 -> x0, loops' own time: 26.6 us -> none  [the longest x2 24.1 us: conv_rows(): pieces = lax.map(slab_term, jnp.arange(loop_turns, dtype=jnp.int32))]
    pallas_call x0 -> x1, Pallas kernels: none -> 18.7 us  [convolutions(): pl.pallas_call(conv_kernel, out_shape=(jax.ShapeDtypeStruct((4096, 256),...]
    squeeze x48 -> x0, local copies, waits for them, and re-layouts: 6.87 us -> none  [slab_term(): kernel[offset_x, 0:tap_group].reshape(tap_group * in_width, out_width)]
  transfers between devices with their start and end apart: 9 -> 9, of which waited for: 4 -> 5; matrix products, arithmetic and copies ran while one was open for 53% -> 3% of each run, Pallas kernels for 0% -> 0%
where the time goes in v1:
time: 298 us
  waiting for transfers between devices  249 us (84%)
  Pallas kernels  18.7 us (6%)
  between operations  13.8 us (5%)
  other arithmetic  9.16 us (3%)
  starting transfers between devices  5.33 us (2%)
    reduce_scatter x1, waiting for transfers between devices, local(): lax.psum_scatter(pf.reshape(64, 64, 256), 'chan', scatter_dimension=0, ti...  84.7 us
    all_gather x1, waiting for transfers between devices, local(): uv = with_halo(lax.all_gather(upstream, 'chan', axis=0, tiled=True))  48 us
    reduce_scatter x1, waiting for transfers between devices, local(): lax.psum_scatter(pd.reshape(64, 32, 256), 'filt', scatter_dimension=0, ti...  44 us
    all_gather x1, waiting for transfers between devices, local(): xv = with_halo(lax.all_gather(voxels, 'filt', axis=0, tiled=True))  41.5 us
    psum x1, waiting for transfers between devices, local(): filter_grad = lax.psum(dw, 'space') / jnp.sqrt(jnp.float32(128 * 256))  28.5 us
    pallas_call x1, Pallas kernels, convolutions(): pl.pallas_call(conv_kernel, out_shape=(jax.ShapeDtypeStruct((4096, 256),...  18.7 us
  transfers between devices with their start and end apart: 9, of which 5 were waited for; matrix products, arithmetic and copies ran while one was open for 3% of the time, Pallas kernels for 0%

profile of v1, /device:TPU:32, one launch (start us, length us, event | category | flops | bytes accessed | tf_op | source)
XLA Modules:
  0.0 297.9 jit_solution(5781694655575393610)
XLA Ops:
  7.2 0.0 all-gather.3.cloned.1.call-start
  7.2 0.7 all-gather.3.cloned.1.call-update
  7.9 0.0 all-gather.5.cloned.1.call-start
  7.9 0.7 all-gather.5.cloned.1.call-update
  8.6 0.0 all-reduce.2.cloned.1.call-start
  8.7 41.5 %all-gather.3.cloned.1.call-done = bf16[64,32,256]{2,1,0:T(8,128)(2,1)} async-done(((bf16[8,32,256]{2,1,0:T(8,128)(2,1)}), bf16[64,32,256]{2,1,0:T(8,128)(2,1)}) %all-gather.3.cloned.1.call-update) | async-done | bytes 1048592 | tf_op jit(solution)/shard_map/all_gather | solution.py:126
  50.2 0.7 fusion.1
  50.9 1.3 collective-permute-start
  52.2 1.3 collective-permute-start.1
  53.5 48.0 %all-gather.5.cloned.1.call-done = bf16[64,64,256]{2,1,0:T(8,128)(2,1)} async-done(((bf16[4,64,256]{2,1,0:T(8,128)(2,1)}), bf16[64,64,256]{2,1,0:T(8,128)(2,1)}) %all-gather.5.cloned.1.call-update) | async-done | bytes 2097168 | tf_op jit(solution)/shard_map/all_gather | solution.py:127
  101.6 0.0 copy-start
  101.6 0.9 fusion
  102.5 1.3 collective-permute-start.2
  103.8 1.3 collective-permute-start.3
  105.1 0.0 collective-permute-done
  105.1 0.0 collective-permute-done.1
  105.1 2.4 pad_maximum_fusion.1.xv
  107.5 0.0 collective-permute-done.2
  107.6 0.0 collective-permute-done.3
  107.6 0.0 copy-done
  107.6 1.7 pad_maximum_fusion
  109.2 18.7 %shard_map.58 = (f32[4096,256]{1,0:T(8,128)}, f32[2048,256]{1,0:T(8,128)}, f32[27,32,64]{2,1,0:T(8,128)}) custom-call(bf16[66,32,256]{2,1,0:T(8,128)(2,1)} %pad_maximum_fusion.1.xv, bf16[4224,256]{1,0:T(8,128)(2,1)} %bitcast.3, bf16[27,32,64]{2,1,0:T(8,128)(2,1)} %fl.1), custom_call_target="tpu_custom_call" | custom-call | tf_op jit(solution)/shard_map/pallas_call | solution.py:99
  127.9 0.0 all-reduce.2.cloned.1.call-update
  128.0 0.0 reduce-scatter.5.cloned.1.call-start
  128.0 0.5 reduce-scatter.5.cloned.1.call-update
  128.5 0.0 reduce-scatter.3.cloned.1.call-start
  128.6 0.5 reduce-scatter.3.cloned.1.call-update
  129.1 28.5 %all-reduce.2.cloned.1.call-done = f32[27,32,64]{2,1,0:T(8,128)} async-done(((f32[27,32,64]{2,1,0:T(8,128)}), f32[27,32,64]{2,1,0:T(8,128)}) %all-reduce.2.cloned.1.call-update) | async-done | bytes 221200 | tf_op jit(solution)/shard_map/psum | solution.py:131
  157.6 1.8 broadcast_multiply_fusion
  159.4 44.0 %reduce-scatter.5.cloned.1.call-done = f32[8,32,256]{2,1,0:T(8,128)} async-done(((f32[64,32,256]{2,1,0:T(8,128)}), f32[8,32,256]{2,1,0:T(8,128)}) %reduce-scatter.5.cloned.1.call-update) | async-done | bytes 262160 | tf_op jit(solution)/shard_map/reduce_scatter | solution.py:130
  203.5 1.6 convert_element_type.7
  205.1 84.7 %reduce-scatter.3.cloned.1.call-done = f32[4,64,256]{2,1,0:T(8,128)} async-done(((f32[64,64,256]{2,1,0:T(8,128)}), f32[4,64,256]{2,1,0:T(8,128)}) %reduce-scatter.3.cloned.1.call-update) | async-done | bytes 262160 | tf_op jit(solution)/shard_map/reduce_scatter | solution.py:129
  289.8 1.6 convert_element_type.6
Async XLA Ops:
  7.2 43.0 %all-gather.3.cloned.1.call-start = ((), (), s32[]{:S(2)}) async-start(), calls=%async_computation.2 | async-start | bytes 1179648 | tf_op jit(solution)/shard_map/all_gather | solution.py:126
  7.9 93.7 %all-gather.5.cloned.1.call-start = ((), (), s32[]{:S(2)}) async-start(), calls=%async_computation.3 | async-start | bytes 2228224 | tf_op jit(solution)/shard_map/all_gather | solution.py:127
  8.6 149.0 %all-reduce.2.cloned.1.call-start = ((), (), s32[]{:S(2)}) async-start(), calls=%async_computation.6 | async-start | bytes 884736 | tf_op jit(solution)/shard_map/psum | solution.py:131
  50.9 54.1 %collective-permute-start = (bf16[1,32,256]{2,1,0:T(8,128)(2,1)S(1)}, bf16[1,32,256]{2,1,0:T(8,128)(2,1)S(1)}, u32[]{:S(2)}, u32[]{:S(2)}) collective-permute-start(bf16[1,32,256]{2,1,0:T(8,128)(2,1)S(1)} %get-tuple-element.11), channel_id=1, source_target_pairs={{0,1},{2,3},{4,5},{6,7},{8,9},{10,11},{12,13},{14,15},{16,17},{18,... | collective-permute-start | bytes 49160 | tf_op jit(solution)/shard_map/ppermute | solution.py:120
  52.2 52.9 %collective-permute-start.1 = (bf16[1,32,256]{2,1,0:T(8,128)(2,1)S(1)}, bf16[1,32,256]{2,1,0:T(8,128)(2,1)S(1)}, u32[]{:S(2)}, u32[]{:S(2)}) collective-permute-start(bf16[1,32,256]{2,1,0:T(8,128)(2,1)S(1)} %get-tuple-element.12), channel_id=1, source_target_pairs={{1,0},{3,2},{5,4},{7,6},{9,8},{11,10},{13,12},{15,14},{17,16},{19,... | collective-permute-start | bytes 49160 | tf_op jit(solution)/shard_map/ppermute | solution.py:121
  101.6 6.0 %copy-start = (bf16[64,64,256]{2,1,0:T(8,128)(2,1)S(1)}, bf16[64,64,256]{2,1,0:T(8,128)(2,1)}, u32[]{:S(2)}) copy-start(bf16[64,64,256]{2,1,0:T(8,128)(2,1)} %all-gather.5.cloned.1.call-done) | copy-start | bytes 6291460
  102.5 5.1 %collective-permute-start.2 = (bf16[1,64,256]{2,1,0:T(8,128)(2,1)S(1)}, bf16[1,64,256]{2,1,0:T(8,128)(2,1)S(1)}, u32[]{:S(2)}, u32[]{:S(2)}) collective-permute-start(bf16[1,64,256]{2,1,0:T(8,128)(2,1)S(1)} %get-tuple-element.9), channel_id=1, source_target_pairs={{0,1},{2,3},{4,5},{6,7},{8,9},{10,11},{12,13},{14,15},{16,17},{18,... | collective-permute-start | bytes 98312 | tf_op jit(solution)/shard_map/ppermute | solution.py:120
  103.8 3.8 %collective-permute-start.3 = (bf16[1,64,256]{2,1,0:T(8,128)(2,1)S(1)}, bf16[1,64,256]{2,1,0:T(8,128)(2,1)S(1)}, u32[]{:S(2)}, u32[]{:S(2)}) collective-permute-start(bf16[1,64,256]{2,1,0:T(8,128)(2,1)S(1)} %get-tuple-element.10), channel_id=1, source_target_pairs={{1,0},{3,2},{5,4},{7,6},{9,8},{11,10},{13,12},{15,14},{17,16},{19,... | collective-permute-start | bytes 98312 | tf_op jit(solution)/shard_map/ppermute | solution.py:121
  128.0 75.5 %reduce-scatter.5.cloned.1.call-start = ((), (), s32[]{:S(2)}) async-start(), calls=%async_computation.5 | async-start | bytes 2359296 | tf_op jit(solution)/shard_map/reduce_scatter | solution.py:130
  128.5 161.3 %reduce-scatter.3.cloned.1.call-start = ((), (), s32[]{:S(2)}) async-start(), calls=%async_computation.4 | async-start | bytes 4456448 | tf_op jit(solution)/shard_map/reduce_scatter | solution.py:129
Sparse Core Ops, SparseCore 0:
  9.8 40.3 all-gather.2
  52.6 48.8 all-gather.4
  128.1 29.4 all-reduce.1
  160.0 43.4 reduce-scatter.4
  207.0 82.8 reduce-scatter.2

commit v2 on v1

v2 whole, which is shorter than its diff:
```python
import jax
import jax.numpy as jnp
from jax import lax
from jax.experimental import pallas as pl
from jax.experimental.pallas import tpu as pltpu
from jax.sharding import PartitionSpec as P

OFFSETS = [(dy, dz) for dy in (-1, 0, 1) for dz in (-1, 0, 1)]
GROUP = 4
COPIES = 105


def tap_masks():
    lane = lax.broadcasted_iota(jnp.int32, (1, 256), 1)
    z = lane & 15
    y = lane >> 4
    out = []
    for dy, dz in OFFSETS:
        ok = (y + dy >= 0) & (y + dy < 16) & (z + dz >= 0) & (z + dz < 16)
        out.append(jnp.where(ok, 1.0, 0.0).astype(jnp.float32))
    return out


def columns(x, masks, sign):
    parts = []
    for i in range(9):
        dy, dz = OFFSETS[i]
        off = sign * (dy * 16 + dz)
        if off == 0:
            parts.append(x)
            continue
        mask = masks[i if sign > 0 else 8 - i]
        parts.append(pltpu.roll(x, (-off) % 256, 1) * mask.astype(x.dtype))
    return jnp.concatenate(parts, axis=0)


def spread(acc, base, width, ys):
    n = len(ys)
    for i in range(n + 2):
        total = None
        for j in range(max(0, i - 2), min(n, i + 1)):
            part = ys[j][width * (i - j) : width * (i - j + 1), :]
            total = part if total is None else total + part
        acc[base + i] = acc[base + i] + total


def full_kernel(
    vox, fl, up, out_r, out_v, out_w,
    xv, uv, wf, wd, accf, accd, accw, far_1, near_1, far_2, near_2, ring, other_w,
    send_sems, recv_sems,
):
    chan = lax.axis_index("chan")
    z = lax.axis_index("filt")
    core = lax.axis_index("space")
    x = lax.rem(chan, 4)
    y = lax.div(chan, 4)

    def target(axis, step):
        if axis == "z":
            return {"filt": lax.rem(z + step + 8, 8)}
        if axis == "x":
            return {"chan": 4 * y + lax.rem(x + step + 4, 4)}
        if axis == "y":
            return {"chan": 4 * lax.rem(y + step + 4, 4) + x}
        return {"space": 1 - core}

    barrier = pltpu.get_barrier_semaphore()
    for axis, step in (("z", 1), ("z", -1), ("x", 1), ("x", -1), ("y", 1), ("y", -1), ("c", 0)):
        pl.semaphore_signal(
            barrier, inc=1, device_id=target(axis, step), device_id_type=pl.DeviceIdType.MESH
        )
    pl.semaphore_wait(barrier, 7)

    copies = []

    def send(source, dest, axis, step):
        k = len(copies)
        copy = pltpu.make_async_remote_copy(
            src_ref=source,
            dst_ref=dest,
            send_sem=send_sems.at[k],
            recv_sem=recv_sems.at[k],
            device_id=target(axis, step),
            device_id_type=pl.DeviceIdType.MESH,
        )
        copy.start()
        copies.append(copy)
        return copy

    steps = (1, -1)
    axes = (("x", "y"), ("y", "x"))
    place = {"x": x, "y": y}

    def block_at(half, first, second):
        a = lax.rem(place[axes[half][0]] + first + 4, 4)
        b = lax.rem(place[axes[half][1]] + second + 4, 4)
        return (4 * b + a) if half == 0 else (4 * a + b)

    def u_at(half, first, second, plane, count):
        return uv.at[pl.ds(1 + 4 * block_at(half, first, second) + 2 * half + plane, count)]

    def v_at(distance, plane, count):
        return xv.at[pl.ds(1 + 8 * lax.rem(z + distance + 8, 8) + plane, count)]

    z_now = [send(vox, v_at(0, 0, 8), "z", st) for st in steps]
    first_sent = [
        [send(up.at[pl.ds(2 * h, 2)], u_at(h, 0, 0, 0, 2), axes[h][0], st) for st in steps]
        for h in range(2)
    ]
    second_sent = {}
    for h in range(2):
        second_sent[h, 0] = [
            send(up.at[pl.ds(2 * h, 2)], u_at(h, 0, 0, 0, 2), axes[h][1], st) for st in steps
        ]

    xv[pl.ds(1 + 8 * z, 8)] = vox[...]
    uv[pl.ds(1 + 4 * chan, 4)] = up[...]
    xv[65 * core] = jnp.zeros((32, 256), jnp.bfloat16)
    uv[65 * core] = jnp.zeros((64, 256), jnp.bfloat16)
    for a in range(3):
        w = fl[9 * a : 9 * a + 9].reshape(288, 64)
        wf[64 * (2 - a) : 64 * (3 - a), :] = w.astype(jnp.float32).T.astype(jnp.bfloat16)
        for t in range(9):
            wd[32 * a : 32 * a + 32, 64 * t : 64 * t + 64] = fl[9 * a + t]
    accf[...] = jnp.zeros_like(accf)
    accd[...] = jnp.zeros_like(accd)
    accw[...] = jnp.zeros_like(accw)
    masks = tap_masks()

    def z_hop(hop, now):
        later = []
        for i, st in enumerate(steps):
            now[i].wait_recv()
            if hop < 3:
                part = v_at(-st * hop, 0, 8)
            elif hop == 3:
                part = v_at(-st * hop, 4 * i, 4)
            else:
                continue
            later.append(send(part, part, "z", st))
        return later

    def pass_second(h, e):
        second_sent[h, e] = [
            send(u_at(h, e, 0, 0, 2), u_at(h, e, 0, 0, 2), axes[h][1], st) for st in steps
        ]

    last = []

    def pass_on(h, e):
        for i, st in enumerate(steps):
            second_sent[h, e][i].wait_recv()
            part = u_at(h, e, -st, i, 1)
            last.append(send(part, part, axes[h][1], st))

    far_sent = [[], []]
    for h in range(2):
        for i, st in enumerate(steps):
            first_sent[h][i].wait_recv()
            part = u_at(h, -st, 0, i, 1)
            far_sent[h].append(send(part, part, axes[h][0], st))
    for h in range(2):
        for e in (-1, 1):
            pass_second(h, e)
    z_now = z_hop(1, z_now)
    for h in range(2):
        pass_on(h, 0)
    for h in range(2):
        for copy in far_sent[h]:
            copy.wait_recv()
        pass_second(h, 2)
    z_now = z_hop(2, z_now)
    for h in range(2):
        pass_on(h, -1)
        pass_on(h, 1)
    z_now = z_hop(3, z_now)
    for h in range(2):
        pass_on(h, 2)
    z_hop(4, z_now)
    for copy in last:
        copy.wait_recv()
    inner, outer = 64 - 63 * core, 65 * core
    halos = [
        send(xv.at[inner], xv.at[outer], "c", 0),
        send(uv.at[inner], uv.at[outer], "c", 0),
    ]

    def forward(b):
        cols = [columns(xv[b * GROUP + j + 1], masks, 1) for j in range(GROUP)]
        ys = [jnp.dot(wf[...], c, preferred_element_type=jnp.float32) for c in cols]
        spread(accf, b * GROUP + 1, 64, ys)
        around = [uv[pl.ds(b * GROUP + j, 3)].reshape(192, 256) for j in range(GROUP)]
        accw[...] = accw[...] + lax.dot_general(
            jnp.concatenate(cols, axis=1),
            jnp.concatenate(around, axis=1),
            (((1,), (1,)), ((), ())),
            preferred_element_type=jnp.float32,
        )

    def backward(b):
        ys = [
            jnp.dot(
                wd[...],
                columns(uv[b * GROUP + j + 1], masks, -1),
                preferred_element_type=jnp.float32,
            )
            for j in range(GROUP)
        ]
        spread(accd, b * GROUP + 1, 32, ys)

    for copy in halos:
        copy.wait_recv()
    for q in (0, 65):
        spread(accf, q, 64, [jnp.dot(wf[...], columns(xv[q], masks, 1), preferred_element_type=jnp.float32)])
        spread(accd, q, 32, [jnp.dot(wd[...], columns(uv[q], masks, -1), preferred_element_type=jnp.float32)])

    @pl.loop(0, 64 // GROUP)
    def _(b):
        forward(b)
        backward(b)

    def d_at(distance, part):
        return accd.at[pl.ds(2 + 8 * lax.rem(z + distance + 8, 8) + 4 * part, 4)]

    ring_sent = [[], []]

    def ring_send(i, j):
        part = (i + j) % 2
        ring_sent[i].append(
            send(d_at(steps[i] * (4 - (j + 1) // 2), part), ring.at[i, j], "z", steps[i])
        )

    def ring_take(j):
        for i in range(2):
            ring_sent[i][j].wait_recv()
            held = d_at(steps[i] * (3 - (j + 1) // 2), (i + j) % 2)
            held[...] = held[...] + ring[i, j]
            if j < 5:
                ring_send(i, j + 2)

    def f_at(half, first, second, plane, count):
        return accf.at[pl.ds(2 + 4 * block_at(1 - half, first, second) + 2 * half + plane, count)]

    far_copies, near_copies = {}, {}

    def far_send(h, d):
        for i, st in enumerate(steps):
            far_copies[h, d, i] = send(
                f_at(h, 2, d, i, 1), far_1.at[h, i, pl.ds(d, 1)], axes[1 - h][0], st
            )

    def far_take(h, d):
        for i, st in enumerate(steps):
            far_copies[h, d, i].wait_recv()
            held = f_at(h, st, d, i, 1)
            held[...] = held[...] + far_1[h, i, pl.ds(d, 1)]
            near_copies[h, d, i] = send(
                f_at(h, st, d, 0, 2), near_1.at[h, i, d], axes[1 - h][0], st
            )

    def near_take(h, d):
        for i in range(2):
            near_copies[h, d, i].wait_recv()
        held = f_at(h, 0, d, 0, 2)
        held[...] = held[...] + near_1[h, 0, d] + near_1[h, 1, d]

    for i in range(2):
        ring_send(i, 0)
        ring_send(i, 1)
    order = (2, 1, 3, 0)
    for d in order:
        for h in range(2):
            far_send(h, d)
    w_copy = send(accw, other_w, "c", 0)
    for j, d in enumerate(order):
        for h in range(2):
            far_take(h, d)
        ring_take(j)
    second_far, second_near = {}, {}
    for h in range(2):
        near_take(h, 2)
        for i, st in enumerate(steps):
            second_far[h, i] = send(
                f_at(h, 0, 2, i, 1), far_2.at[h, pl.ds(i, 1)], axes[1 - h][1], st
            )
    ring_take(4)
    for i, d in ((0, 1), (1, 3)):
        for h in range(2):
            near_take(h, d)
    for i, st in enumerate(steps):
        for h in range(2):
            second_far[h, i].wait_recv()
            held = f_at(h, 0, st, i, 1)
            held[...] = held[...] + far_2[h, pl.ds(i, 1)]
            second_near[h, i] = send(f_at(h, 0, st, 0, 2), near_2.at[h, i], axes[1 - h][1], st)
    ring_take(5)
    for h in range(2):
        near_take(h, 0)
    w_copy.wait_recv()
    other_w[...] = (other_w[...] + accw[...]) / jnp.sqrt(jnp.float32(128 * 256))
    for a in range(3):
        for t in range(9):
            out_w[9 * a + t] = other_w[32 * t : 32 * t + 32, 64 * (2 - a) : 64 * (3 - a)]
    ring_take(6)
    out_v[...] = accd[pl.ds(2 + 8 * z, 8)].astype(jnp.bfloat16)
    for h in range(2):
        for i in range(2):
            second_near[h, i].wait_recv()
        total = f_at(h, 0, 0, 0, 2)[...] + near_2[h, 0] + near_2[h, 1]
        out_r[2 * h : 2 * h + 2] = total.astype(jnp.bfloat16)
    for copy in copies:
        copy.wait_send()


def local(voxels, filters, upstream):
    f32, bf16 = jnp.float32, jnp.bfloat16
    return pl.pallas_call(
        full_kernel,
        out_shape=(
            jax.ShapeDtypeStruct((4, 64, 256), bf16),
            jax.ShapeDtypeStruct((8, 32, 256), bf16),
            jax.ShapeDtypeStruct((27, 32, 64), f32),
        ),
        in_specs=[pl.BlockSpec(memory_space=pltpu.VMEM)] * 3,
        out_specs=[pl.BlockSpec(memory_space=pltpu.VMEM)] * 3,
        scratch_shapes=[
            pltpu.VMEM((66, 32, 256), bf16),
            pltpu.VMEM((66, 64, 256), bf16),
            pltpu.VMEM((192, 288), bf16),
            pltpu.VMEM((96, 576), bf16),
            pltpu.VMEM((68, 64, 256), f32),
            pltpu.VMEM((68, 32, 256), f32),
            pltpu.VMEM((288, 192), f32),
            pltpu.VMEM((2, 2, 4, 64, 256), f32),
            pltpu.VMEM((2, 2, 4, 2, 64, 256), f32),
            pltpu.VMEM((2, 2, 64, 256), f32),
            pltpu.VMEM((2, 2, 2, 64, 256), f32),
            pltpu.VMEM((2, 7, 4, 32, 256), f32),
            pltpu.VMEM((288, 192), f32),
            pltpu.SemaphoreType.DMA((COPIES,)),
            pltpu.SemaphoreType.DMA((COPIES,)),
        ],
        compiler_params=pltpu.CompilerParams(
            collective_id=0, has_side_effects=True, vmem_limit_bytes=60 * 2**20
        ),
    )(voxels, filters, upstream)


def solution(mesh):
    return jax.shard_map(
        local,
        mesh=mesh,
        in_specs=(
            P(("space", "filt"), "chan", None),
            P(None, "chan", "filt"),
            P(("space", "chan"), "filt", None),
        ),
        out_specs=(
            P(("space", "chan"), "filt", None),
            P(("space", "filt"), "chan", None),
            P(None, "chan", "filt"),
        ),
        check_vma=False,
    )
```

time: 298 us -> 75.2 us (0.25)
  waiting for transfers between devices: 249 us -> 0 us
  Pallas kernels: 18.7 us -> 69.8 us
  between operations: 13.8 us -> 0.65 us
  other arithmetic: 9.16 us -> 0 us
  starting transfers between devices: 5.33 us -> 0 us
    reduce_scatter x2 -> x0, waiting for transfers between devices: 129 us -> none  [the longest x1 84.7 us: local(): lax.psum_scatter(pf.reshape(64, 64, 256), 'chan', scatter_dimension=0, ti...]
    all_gather x2 -> x0, waiting for transfers between devices: 89.5 us -> none  [the longest x1 48 us: local(): uv = with_halo(lax.all_gather(upstream, 'chan', axis=0, tiled=True))]
    pallas_call x1, Pallas kernels: 18.7 us -> 69.8 us  [local(): pl.pallas_call(full_kernel, out_shape=(jax.ShapeDtypeStruct((4, 64, 256),...]
    psum x1 -> x0, waiting for transfers between devices: 28.5 us -> none  [local(): filter_grad = lax.psum(dw, 'space') / jnp.sqrt(jnp.float32(128 * 256))]
    ppermute x4 -> x0, starting transfers between devices: 5.14 us -> none  [the longest x2 2.58 us: with_halo(): high = lax.ppermute(block[:1], 'space', [(1, 0)])]
    concatenate x2 -> x0, other arithmetic: 4.11 us -> none  [with_halo(): return jnp.concatenate([low, block, high], axis=0)]
    unnamed x2 -> x5, local copies, waits for them, and re-layouts: 0.01 us -> 3.95 us
    convert_element_type x2 -> x0, other arithmetic: 3.24 us -> none  [the longest x1 1.62 us: local(): voxel_grad.astype(jnp.bfloat16)]
  transfers between devices with their start and end apart: 9 -> 0, of which waited for: 5 -> 0; matrix products, arithmetic and copies ran while one was open for 3% -> 0% of each run, Pallas kernels for 0% -> 0%
where the time goes in v2:
time: 75.2 us; the launch traced here: 74.4 us
  Pallas kernels  69.8 us (93%)
  local copies, waits for them, and re-layouts  3.95 us (5%)
    pallas_call x1, Pallas kernels, local(): pl.pallas_call(full_kernel, out_shape=(jax.ShapeDtypeStruct((4, 64, 256),...  69.8 us
    unnamed x5, local copies, waits for them, and re-layouts  3.95 us

profile of v2, /device:TPU:32, one launch (start us, length us, event | category | flops | bytes accessed | tf_op | source)
XLA Modules:
  0.0 74.4 jit_solution(8134890533461132570)
XLA Ops:
  0.6 69.8 %shard_map.58 = (bf16[4,64,256]{2,1,0:T(8,128)(2,1)}, bf16[8,32,256]{2,1,0:T(8,128)(2,1)}, f32[27,32,64]{2,1,0:T(8,128)}) custom-call(bf16[8,32,256]{2,1,0:T(8,128)(2,1)} %vox.1, bf16[27,32,64]{2,1,0:T(8,128)(2,1)} %fl.1, bf16[4,64,256]{2,1,0:T(8,128)(2,1)} %up.1), custom_call_target="tpu_custom_call" | custom-call | tf_op jit(solution)/shard_map/pallas_call | solution.py:317
  70.4 0.0 copy-start
  70.4 1.6 %copy.9 = bf16[4,64,256]{2,1,0:T(8,128)(2,1)} copy(bf16[4,64,256]{2,1,0:T(8,128)(2,1)} %get-tuple-element.6) | data formatting | bytes 262144
  72.0 1.6 %copy.10 = bf16[8,32,256]{2,1,0:T(8,128)(2,1)} copy(bf16[8,32,256]{2,1,0:T(8,128)(2,1)} %get-tuple-element.7) | data formatting | bytes 262144
  73.6 0.0 copy-done
  73.6 0.8 %copy.11 = f32[27,32,64]{2,1,0:T(8,128)} copy(f32[27,32,64]{2,1,0:T(8,128)S(1)} %copy-done) | data formatting | bytes 442368
Async XLA Ops:
  70.4 3.2 %copy-start = (f32[27,32,64]{2,1,0:T(8,128)S(1)}, f32[27,32,64]{2,1,0:T(8,128)}, u32[]{:S(2)}) copy-start(f32[27,32,64]{2,1,0:T(8,128)} %get-tuple-element.8) | copy-start | bytes 663556

commit v3 on v2

--- a/solution.py
+++ b/solution.py
@@ -153,6 +153,46 @@
             part = u_at(h, e, -st, i, 1)
             last.append(send(part, part, axes[h][1], st))
 
+    def forward(p0):
+        ys = [
+            jnp.dot(wf[...], columns(xv[p0 + j], masks, 1), preferred_element_type=jnp.float32)
+            for j in range(8)
+        ]
+        spread(accf, p0, 64, ys)
+
+    def backward(starts):
+        found = [
+            [
+                jnp.dot(
+                    wd[...], columns(uv[p0 + j], masks, -1), preferred_element_type=jnp.float32
+                )
+                for j in range(4)
+            ]
+            for p0 in starts
+        ]
+        for p0, ys in zip(starts, found):
+            spread(accd, p0, 32, ys)
+
+    def forward_at(hop):
+        @pl.loop(0, 2)
+        def _(k):
+            forward(1 + 8 * lax.rem(z + hop * (1 - 2 * k) + 8, 8))
+
+    def u_start(dx, dy):
+        return 1 + 4 * (4 * lax.rem(y + dy + 4, 4) + lax.rem(x + dx + 4, 4))
+
+    def weights(low, high):
+        @pl.loop(low, high)
+        def _(b):
+            cols = [columns(xv[b * GROUP + j + 1], masks, 1) for j in range(GROUP)]
+            around = [uv[pl.ds(b * GROUP + j, 3)].reshape(192, 256) for j in range(GROUP)]
+            accw[...] = accw[...] + lax.dot_general(
+                jnp.concatenate(cols, axis=1),
+                jnp.concatenate(around, axis=1),
+                (((1,), (1,)), ((), ())),
+                preferred_element_type=jnp.float32,
+            )
+
     far_sent = [[], []]
     for h in range(2):
         for i, st in enumerate(steps):
@@ -162,6 +202,7 @@
     for h in range(2):
         for e in (-1, 1):
             pass_second(h, e)
+    forward(1 + 8 * z)
     z_now = z_hop(1, z_now)
     for h in range(2):
         pass_on(h, 0)
@@ -169,55 +210,37 @@
         for copy in far_sent[h]:
             copy.wait_recv()
         pass_second(h, 2)
+    forward_at(1)
     z_now = z_hop(2, z_now)
     for h in range(2):
         pass_on(h, -1)
         pass_on(h, 1)
+    backward([u_start(0, 0)])
+
+    @pl.loop(0, 2)
+    def _(k):
+        backward([u_start(1 - 2 * k, 0), u_start(0, 1 - 2 * k)])
+
+    forward_at(2)
     z_now = z_hop(3, z_now)
     for h in range(2):
         pass_on(h, 2)
+    forward_at(3)
+
+    @pl.loop(0, 2)
+    def _(k):
+        backward([u_start(1 - 2 * k, 1), u_start(1 - 2 * k, -1)])
+
     z_hop(4, z_now)
+    inner, outer = 64 - 63 * core, 65 * core
+    x_halo = send(xv.at[inner], xv.at[outer], "c", 0)
+    forward(1 + 8 * lax.rem(z + 4, 8))
     for copy in last:
         copy.wait_recv()
-    inner, outer = 64 - 63 * core, 65 * core
-    halos = [
-        send(xv.at[inner], xv.at[outer], "c", 0),
-        send(uv.at[inner], uv.at[outer], "c", 0),
-    ]
-
-    def forward(b):
-        cols = [columns(xv[b * GROUP + j + 1], masks, 1) for j in range(GROUP)]
-        ys = [jnp.dot(wf[...], c, preferred_element_type=jnp.float32) for c in cols]
-        spread(accf, b * GROUP + 1, 64, ys)
-        around = [uv[pl.ds(b * GROUP + j, 3)].reshape(192, 256) for j in range(GROUP)]
-        accw[...] = accw[...] + lax.dot_general(
-            jnp.concatenate(cols, axis=1),
-            jnp.concatenate(around, axis=1),
-            (((1,), (1,)), ((), ())),
-            preferred_element_type=jnp.float32,
-        )
-
-    def backward(b):
-        ys = [
-            jnp.dot(
-                wd[...],
-                columns(uv[b * GROUP + j + 1], masks, -1),
-                preferred_element_type=jnp.float32,
-            )
-            for j in range(GROUP)
-        ]
-        spread(accd, b * GROUP + 1, 32, ys)
-
-    for copy in halos:
-        copy.wait_recv()
+    u_halo = send(uv.at[inner], uv.at[outer], "c", 0)
+    x_halo.wait_recv()
     for q in (0, 65):
         spread(accf, q, 64, [jnp.dot(wf[...], columns(xv[q], masks, 1), preferred_element_type=jnp.float32)])
-        spread(accd, q, 32, [jnp.dot(wd[...], columns(uv[q], masks, -1), preferred_element_type=jnp.float32)])
-
-    @pl.loop(0, 64 // GROUP)
-    def _(b):
-        forward(b)
-        backward(b)
 
     def d_at(distance, part):
         return accd.at[pl.ds(2 + 8 * lax.rem(z + distance + 8, 8) + 4 * part, 4)]
@@ -264,18 +287,29 @@
         held = f_at(h, 0, d, 0, 2)
         held[...] = held[...] + near_1[h, 0, d] + near_1[h, 1, d]
 
-    for i in range(2):
-        ring_send(i, 0)
-        ring_send(i, 1)
     order = (2, 1, 3, 0)
     for d in order:
         for h in range(2):
             far_send(h, d)
-    w_copy = send(accw, other_w, "c", 0)
-    for j, d in enumerate(order):
+
+    @pl.loop(0, 3)
+    def _(k):
+        t = k + lax.div(k, 2)
+        backward([u_start(2, t), u_start(t, 2)])
+
+    backward([u_start(2, 2)])
+    u_halo.wait_recv()
+    for q in (0, 65):
+        spread(accd, q, 32, [jnp.dot(wd[...], columns(uv[q], masks, -1), preferred_element_type=jnp.float32)])
+    for i in range(2):
+        ring_send(i, 0)
+        ring_send(i, 1)
+    for d, low in ((2, 0), (1, 0), (3, 2), (0, 4)):
         for h in range(2):
             far_take(h, d)
-        ring_take(j)
+        if d != 2:
+            weights(low, low + 2)
+    ring_take(0)
     second_far, second_near = {}, {}
     for h in range(2):
         near_take(h, 2)
@@ -283,31 +317,39 @@
             second_far[h, i] = send(
                 f_at(h, 0, 2, i, 1), far_2.at[h, pl.ds(i, 1)], axes[1 - h][1], st
             )
-    ring_take(4)
-    for i, d in ((0, 1), (1, 3)):
-        for h in range(2):
-            near_take(h, d)
+    weights(6, 9)
+    ring_take(1)
+    for h in range(2):
+        near_take(h, 1)
+    weights(9, 12)
+    ring_take(2)
+    for h in range(2):
+        near_take(h, 3)
     for i, st in enumerate(steps):
         for h in range(2):
             second_far[h, i].wait_recv()
             held = f_at(h, 0, st, i, 1)
             held[...] = held[...] + far_2[h, pl.ds(i, 1)]
             second_near[h, i] = send(f_at(h, 0, st, 0, 2), near_2.at[h, i], axes[1 - h][1], st)
-    ring_take(5)
+    weights(12, 16)
+    w_copy = send(accw, other_w, "c", 0)
+    ring_take(3)
     for h in range(2):
         near_take(h, 0)
+    ring_take(4)
     w_copy.wait_recv()
     other_w[...] = (other_w[...] + accw[...]) / jnp.sqrt(jnp.float32(128 * 256))
     for a in range(3):
         for t in range(9):
             out_w[9 * a + t] = other_w[32 * t : 32 * t + 32, 64 * (2 - a) : 64 * (3 - a)]
-    ring_take(6)
-    out_v[...] = accd[pl.ds(2 + 8 * z, 8)].astype(jnp.bfloat16)
+    ring_take(5)
     for h in range(2):
         for i in range(2):
             second_near[h, i].wait_recv()
         total = f_at(h, 0, 0, 0, 2)[...] + near_2[h, 0] + near_2[h, 1]
         out_r[2 * h : 2 * h + 2] = total.astype(jnp.bfloat16)
+    ring_take(6)
+    out_v[...] = accd[pl.ds(2 + 8 * z, 8)].astype(jnp.bfloat16)
     for copy in copies:
         copy.wait_send()
 

time: 75.2 us -> 66.3 us (0.88)
  Pallas kernels: 69.8 us -> 61.1 us
    pallas_call x1, Pallas kernels: 69.8 us -> 61.1 us  [local(): pl.pallas_call(full_kernel, out_shape=(jax.ShapeDtypeStruct((4, 64, 256),...]
where the time goes in v3:
time: 66.3 us; the launch traced here: 65.7 us
  Pallas kernels  61.1 us (92%)
  local copies, waits for them, and re-layouts  3.95 us (6%)
    pallas_call x1, Pallas kernels, local(): pl.pallas_call(full_kernel, out_shape=(jax.ShapeDtypeStruct((4, 64, 256),...  61.1 us
    unnamed x5, local copies, waits for them, and re-layouts  3.95 us

profile of v3, /device:TPU:32, one launch (start us, length us, event | category | flops | bytes accessed | tf_op | source)
XLA Modules:
  0.0 65.7 jit_solution(9756564952518636981)
XLA Ops:
  0.6 61.1 %shard_map.58 = (bf16[4,64,256]{2,1,0:T(8,128)(2,1)}, bf16[8,32,256]{2,1,0:T(8,128)(2,1)}, f32[27,32,64]{2,1,0:T(8,128)}) custom-call(bf16[8,32,256]{2,1,0:T(8,128)(2,1)} %vox.1, bf16[27,32,64]{2,1,0:T(8,128)(2,1)} %fl.1, bf16[4,64,256]{2,1,0:T(8,128)(2,1)} %up.1), custom_call_target="tpu_custom_call" | custom-call | tf_op jit(solution)/shard_map/pallas_call | solution.py:359
  61.7 0.0 copy-start
  61.7 1.6 %copy.9 = bf16[4,64,256]{2,1,0:T(8,128)(2,1)} copy(bf16[4,64,256]{2,1,0:T(8,128)(2,1)} %get-tuple-element.6) | data formatting | bytes 262144
  63.3 1.6 %copy.10 = bf16[8,32,256]{2,1,0:T(8,128)(2,1)} copy(bf16[8,32,256]{2,1,0:T(8,128)(2,1)} %get-tuple-element.7) | data formatting | bytes 262144
  64.9 0.0 copy-done
  64.9 0.8 %copy.11 = f32[27,32,64]{2,1,0:T(8,128)} copy(f32[27,32,64]{2,1,0:T(8,128)S(1)} %copy-done) | data formatting | bytes 442368
Async XLA Ops:
  61.7 3.2 %copy-start = (f32[27,32,64]{2,1,0:T(8,128)S(1)}, f32[27,32,64]{2,1,0:T(8,128)}, u32[]{:S(2)}) copy-start(f32[27,32,64]{2,1,0:T(8,128)} %get-tuple-element.8) | copy-start | bytes 663556

commit v4 on v3

--- a/solution.py
+++ b/solution.py
@@ -7,7 +7,7 @@
 
 OFFSETS = [(dy, dz) for dy in (-1, 0, 1) for dz in (-1, 0, 1)]
 GROUP = 4
-COPIES = 105
+COPIES = 145
 
 
 def tap_masks():
@@ -102,16 +102,26 @@
     def v_at(distance, plane, count):
         return xv.at[pl.ds(1 + 8 * lax.rem(z + distance + 8, 8) + plane, count)]
 
-    z_now = [send(vox, v_at(0, 0, 8), "z", st) for st in steps]
-    first_sent = [
-        [send(up.at[pl.ds(2 * h, 2)], u_at(h, 0, 0, 0, 2), axes[h][0], st) for st in steps]
-        for h in range(2)
-    ]
-    second_sent = {}
-    for h in range(2):
-        second_sent[h, 0] = [
-            send(up.at[pl.ds(2 * h, 2)], u_at(h, 0, 0, 0, 2), axes[h][1], st) for st in steps
-        ]
+    first_sent, second_sent = {}, {}
+    for turn in range(2):
+        for h in range(2):
+            for i, st in enumerate(steps):
+                n = (i + turn) % 2
+                first_sent[h, i, n] = send(
+                    up.at[pl.ds(2 * h + n, 1)], u_at(h, 0, 0, n, 1), axes[h][0], st
+                )
+    z_sent = {}
+    for n in range(4):
+        for i, st in enumerate(steps):
+            part = n if i == 0 else 3 - n
+            z_sent[1, i, n] = send(vox.at[pl.ds(2 * part, 2)], v_at(0, 2 * part, 2), "z", st)
+    for turn in range(2):
+        for h in range(2):
+            for i, st in enumerate(steps):
+                n = (i + turn) % 2
+                second_sent[h, 0, i, n] = send(
+                    up.at[pl.ds(2 * h + n, 1)], u_at(h, 0, 0, n, 1), axes[h][1], st
+                )
 
     xv[pl.ds(1 + 8 * z, 8)] = vox[...]
     uv[pl.ds(1 + 4 * chan, 4)] = up[...]
@@ -127,31 +137,35 @@
     accw[...] = jnp.zeros_like(accw)
     masks = tap_masks()
 
-    def z_hop(hop, now):
-        later = []
-        for i, st in enumerate(steps):
-            now[i].wait_recv()
-            if hop < 3:
-                part = v_at(-st * hop, 0, 8)
-            elif hop == 3:
-                part = v_at(-st * hop, 4 * i, 4)
-            else:
-                continue
-            later.append(send(part, part, "z", st))
-        return later
+    def z_hop(hop, pieces):
+        for n in pieces:
+            for i, st in enumerate(steps):
+                if hop == 4 and n > 1:
+                    continue
+                z_sent[hop, i, n].wait_recv()
+                if hop == 4 or (hop == 3 and n > 1):
+                    continue
+                piece = v_at(-st * hop, 2 * (n if i == 0 else 3 - n), 2)
+                z_sent[hop + 1, i, n] = send(piece, piece, "z", st)
 
     def pass_second(h, e):
-        second_sent[h, e] = [
-            send(u_at(h, e, 0, 0, 2), u_at(h, e, 0, 0, 2), axes[h][1], st) for st in steps
-        ]
+        for turn in range(2):
+            for i, st in enumerate(steps):
+                n = (i + turn) % 2
+                part = u_at(h, e, 0, n, 1)
+                second_sent[h, e, i, n] = send(part, part, axes[h][1], st)
 
     last = []
 
     def pass_on(h, e):
         for i, st in enumerate(steps):
-            second_sent[h, e][i].wait_recv()
+            second_sent[h, e, i, i].wait_recv()
             part = u_at(h, e, -st, i, 1)
             last.append(send(part, part, axes[h][1], st))
+
+    def rest_of(h, e):
+        for i in range(2):
+            second_sent[h, e, i, 1 - i].wait_recv()
 
     def forward(p0):
         ys = [
@@ -196,45 +210,54 @@
     far_sent = [[], []]
     for h in range(2):
         for i, st in enumerate(steps):
-            first_sent[h][i].wait_recv()
+            first_sent[h, i, i].wait_recv()
             part = u_at(h, -st, 0, i, 1)
             far_sent[h].append(send(part, part, axes[h][0], st))
     for h in range(2):
-        for e in (-1, 1):
-            pass_second(h, e)
+        for i in range(2):
+            first_sent[h, i, 1 - i].wait_recv()
+    for h in range(2):
+        pass_second(h, -1)
+        pass_second(h, 1)
+    z_hop(1, (0, 1))
+    for h in range(2):
+        pass_on(h, 0)
+    z_hop(1, (2, 3))
     forward(1 + 8 * z)
-    z_now = z_hop(1, z_now)
-    for h in range(2):
-        pass_on(h, 0)
     for h in range(2):
         for copy in far_sent[h]:
             copy.wait_recv()
         pass_second(h, 2)
-    forward_at(1)
-    z_now = z_hop(2, z_now)
+    z_hop(2, (0, 1))
+    forward(1 + 8 * lax.rem(z + 1, 8))
+    z_hop(2, (2, 3))
     for h in range(2):
         pass_on(h, -1)
+    forward(1 + 8 * lax.rem(z + 7, 8))
+    z_hop(3, (0, 1))
+    for h in range(2):
         pass_on(h, 1)
+    forward(1 + 8 * lax.rem(z + 2, 8))
+    z_hop(3, (2, 3))
+    for h in range(2):
+        pass_on(h, 2)
+    forward(1 + 8 * lax.rem(z + 6, 8))
+    forward_at(3)
+    z_hop(4, (0, 1))
+    inner, outer = 64 - 63 * core, 65 * core
+    x_halo = send(xv.at[inner], xv.at[outer], "c", 0)
+    forward(1 + 8 * lax.rem(z + 4, 8))
+    for h in range(2):
+        rest_of(h, 0)
     backward([u_start(0, 0)])
 
     @pl.loop(0, 2)
     def _(k):
         backward([u_start(1 - 2 * k, 0), u_start(0, 1 - 2 * k)])
 
-    forward_at(2)
-    z_now = z_hop(3, z_now)
-    for h in range(2):
-        pass_on(h, 2)
-    forward_at(3)
-
-    @pl.loop(0, 2)
-    def _(k):
-        backward([u_start(1 - 2 * k, 1), u_start(1 - 2 * k, -1)])
-
-    z_hop(4, z_now)
-    inner, outer = 64 - 63 * core, 65 * core
-    x_halo = send(xv.at[inner], xv.at[outer], "c", 0)
-    forward(1 + 8 * lax.rem(z + 4, 8))
+    for h in range(2):
+        for e in (-1, 1, 2):
+            rest_of(h, e)
     for copy in last:
         copy.wait_recv()
     u_halo = send(uv.at[inner], uv.at[outer], "c", 0)
@@ -292,6 +315,13 @@
         for h in range(2):
             far_send(h, d)
 
+    @pl.loop(0, 2)
+    def _(k):
+        backward([u_start(1 - 2 * k, 1), u_start(1 - 2 * k, -1)])
+
+    for h in range(2):
+        far_take(h, 2)
+
     @pl.loop(0, 3)
     def _(k):
         t = k + lax.div(k, 2)
@@ -304,12 +334,10 @@
     for i in range(2):
         ring_send(i, 0)
         ring_send(i, 1)
-    for d, low in ((2, 0), (1, 0), (3, 2), (0, 4)):
+    for d in (1, 3):
         for h in range(2):
             far_take(h, d)
-        if d != 2:
-            weights(low, low + 2)
-    ring_take(0)
+    weights(0, 2)
     second_far, second_near = {}, {}
     for h in range(2):
         near_take(h, 2)
@@ -317,6 +345,10 @@
             second_far[h, i] = send(
                 f_at(h, 0, 2, i, 1), far_2.at[h, pl.ds(i, 1)], axes[1 - h][1], st
             )
+    for h in range(2):
+        far_take(h, 0)
+    ring_take(0)
+    weights(2, 6)
     weights(6, 9)
     ring_take(1)
     for h in range(2):

time: 66.3 us -> 64.8 us (0.977)
  Pallas kernels: 61.1 us -> 60 us
    pallas_call x1, Pallas kernels: 61.1 us -> 60 us  [local(): pl.pallas_call(full_kernel, out_shape=(jax.ShapeDtypeStruct((4, 64, 256),...]
where the time goes in v4:
time: 64.8 us; the launch traced here: 64.6 us
  Pallas kernels  60 us (93%)
  local copies, waits for them, and re-layouts  3.95 us (6%)
  between operations  0.65 us (1%)
    pallas_call x1, Pallas kernels, local(): pl.pallas_call(full_kernel, out_shape=(jax.ShapeDtypeStruct((4, 64, 256),...  60 us
    unnamed x5, local copies, waits for them, and re-layouts  3.95 us

profile of v4, /device:TPU:32, one launch (start us, length us, event | category | flops | bytes accessed | tf_op | source)
XLA Modules:
  0.0 64.6 jit_solution(13802708035095843708)
XLA Ops:
  0.6 60.0 %shard_map.58 = (bf16[4,64,256]{2,1,0:T(8,128)(2,1)}, bf16[8,32,256]{2,1,0:T(8,128)(2,1)}, f32[27,32,64]{2,1,0:T(8,128)}) custom-call(bf16[8,32,256]{2,1,0:T(8,128)(2,1)} %vox.1, bf16[27,32,64]{2,1,0:T(8,128)(2,1)} %fl.1, bf16[4,64,256]{2,1,0:T(8,128)(2,1)} %up.1), custom_call_target="tpu_custom_call" | custom-call | tf_op jit(solution)/shard_map/pallas_call | solution.py:391
  60.6 0.0 copy-start
  60.6 1.6 %copy.9 = bf16[4,64,256]{2,1,0:T(8,128)(2,1)} copy(bf16[4,64,256]{2,1,0:T(8,128)(2,1)} %get-tuple-element.6) | data formatting | bytes 262144
  62.3 1.6 %copy.10 = bf16[8,32,256]{2,1,0:T(8,128)(2,1)} copy(bf16[8,32,256]{2,1,0:T(8,128)(2,1)} %get-tuple-element.7) | data formatting | bytes 262144
  63.8 0.0 copy-done
  63.8 0.8 %copy.11 = f32[27,32,64]{2,1,0:T(8,128)} copy(f32[27,32,64]{2,1,0:T(8,128)S(1)} %copy-done) | data formatting | bytes 442368
Async XLA Ops:
  60.6 3.2 %copy-start = (f32[27,32,64]{2,1,0:T(8,128)S(1)}, f32[27,32,64]{2,1,0:T(8,128)}, u32[]{:S(2)}) copy-start(f32[27,32,64]{2,1,0:T(8,128)} %get-tuple-element.8) | copy-start | bytes 663556

commit v5 on v4

--- a/solution.py
+++ b/solution.py
@@ -370,10 +370,7 @@
         near_take(h, 0)
     ring_take(4)
     w_copy.wait_recv()
-    other_w[...] = (other_w[...] + accw[...]) / jnp.sqrt(jnp.float32(128 * 256))
-    for a in range(3):
-        for t in range(9):
-            out_w[9 * a + t] = other_w[32 * t : 32 * t + 32, 64 * (2 - a) : 64 * (3 - a)]
+    out_w[...] = (other_w[...] + accw[...]) / jnp.sqrt(jnp.float32(128 * 256))
     ring_take(5)
     for h in range(2):
         for i in range(2):
@@ -386,14 +383,36 @@
         copy.wait_send()
 
 
+def settle_kernel(r, v, w, out_r, out_v, out_w):
+    out_r[...] = r[...]
+    out_v[...] = v[...]
+    for a in range(3):
+        for t in range(9):
+            out_w[9 * a + t] = w[32 * t : 32 * t + 32, 64 * (2 - a) : 64 * (3 - a)]
+
+
+def settled(responses, voxel_grad, weights):
+    whole = pl.BlockSpec(memory_space=pltpu.VMEM)
+    return pl.pallas_call(
+        settle_kernel,
+        out_shape=(
+            jax.ShapeDtypeStruct(responses.shape, responses.dtype),
+            jax.ShapeDtypeStruct(voxel_grad.shape, voxel_grad.dtype),
+            jax.ShapeDtypeStruct((27, 32, 64), jnp.float32),
+        ),
+        in_specs=[whole] * 3,
+        out_specs=[whole] * 3,
+    )(responses, voxel_grad, weights)
+
+
 def local(voxels, filters, upstream):
     f32, bf16 = jnp.float32, jnp.bfloat16
-    return pl.pallas_call(
+    sums = pl.pallas_call(
         full_kernel,
         out_shape=(
             jax.ShapeDtypeStruct((4, 64, 256), bf16),
             jax.ShapeDtypeStruct((8, 32, 256), bf16),
-            jax.ShapeDtypeStruct((27, 32, 64), f32),
+            jax.ShapeDtypeStruct((288, 192), f32),
         ),
         in_specs=[pl.BlockSpec(memory_space=pltpu.VMEM)] * 3,
         out_specs=[pl.BlockSpec(memory_space=pltpu.VMEM)] * 3,
@@ -418,6 +437,7 @@
             collective_id=0, has_side_effects=True, vmem_limit_bytes=60 * 2**20
         ),
     )(voxels, filters, upstream)
+    return settled(*sums)
 
 
 def solution(mesh):

time: 64.8 us -> 62.7 us (0.968)
  local copies, waits for them, and re-layouts: 3.95 us -> 0 us
  Pallas kernels: 60 us -> 61.9 us
    unnamed x5 -> x0, local copies, waits for them, and re-layouts: 3.95 us -> none
    pallas_call x0 -> x1, Pallas kernels: none -> 1.97 us  [settled(): pl.pallas_call(settle_kernel, out_shape=(jax.ShapeDtypeStruct(responses.s...]
where the time goes in v5:
time: 62.7 us; the launch traced here: 62.5 us
  Pallas kernels  61.9 us (99%)
  between operations  0.64 us (1%)
    pallas_call x1, Pallas kernels, local(): pl.pallas_call(full_kernel, out_shape=(jax.ShapeDtypeStruct((4, 64, 256),...  59.9 us
    pallas_call x1, Pallas kernels, settled(): pl.pallas_call(settle_kernel, out_shape=(jax.ShapeDtypeStruct(responses.s...  1.97 us

profile of v5, /device:TPU:32, one launch (start us, length us, event | category | flops | bytes accessed | tf_op | source)
XLA Modules:
  0.0 62.5 jit_solution(2602519952508267585)
XLA Ops:
  0.6 59.9 %shard_map.58 = (bf16[4,64,256]{2,1,0:T(8,128)(2,1)}, bf16[8,32,256]{2,1,0:T(8,128)(2,1)}, f32[288,192]{1,0:T(8,128)}) custom-call(bf16[8,32,256]{2,1,0:T(8,128)(2,1)} %vox.1, bf16[27,32,64]{2,1,0:T(8,128)(2,1)} %fl.1, bf16[4,64,256]{2,1,0:T(8,128)(2,1)} %up.1), custom_call_target="tpu_custom_call" | custom-call | tf_op jit(solution)/shard_map/pallas_call | solution.py:410
  60.6 2.0 %shard_map.59 = (bf16[4,64,256]{2,1,0:T(8,128)(2,1)}, bf16[8,32,256]{2,1,0:T(8,128)(2,1)}, f32[27,32,64]{2,1,0:T(8,128)}) custom-call(bf16[4,64,256]{2,1,0:T(8,128)(2,1)} %get-tuple-element.6.r, bf16[8,32,256]{2,1,0:T(8,128)(2,1)} %get-tuple-element.7.v, f32[288,192]{1,0:T(8,128)} %get-tuple-element.8.w), custom_call_target="tpu_custom_call" | custom-call | tf_op jit(solution)/shard_map/pallas_call | solution.py:396

commit v6 on v5

--- a/solution.py
+++ b/solution.py
@@ -243,21 +243,28 @@
         pass_on(h, 2)
     forward(1 + 8 * lax.rem(z + 6, 8))
     forward_at(3)
+    for h in range(2):
+        rest_of(h, 0)
+    backward([u_start(0, 0)])
+
+    @pl.loop(0, 2)
+    def _(k):
+        backward([u_start(1 - 2 * k, 0), u_start(0, 1 - 2 * k)])
+
+    for h in range(2):
+        rest_of(h, -1)
+        rest_of(h, 1)
+
+    @pl.loop(0, 2)
+    def _(k):
+        backward([u_start(1 - 2 * k, 1), u_start(1 - 2 * k, -1)])
+
     z_hop(4, (0, 1))
     inner, outer = 64 - 63 * core, 65 * core
     x_halo = send(xv.at[inner], xv.at[outer], "c", 0)
     forward(1 + 8 * lax.rem(z + 4, 8))
     for h in range(2):
-        rest_of(h, 0)
-    backward([u_start(0, 0)])
-
-    @pl.loop(0, 2)
-    def _(k):
-        backward([u_start(1 - 2 * k, 0), u_start(0, 1 - 2 * k)])
-
-    for h in range(2):
-        for e in (-1, 1, 2):
-            rest_of(h, e)
+        rest_of(h, 2)
     for copy in last:
         copy.wait_recv()
     u_halo = send(uv.at[inner], uv.at[outer], "c", 0)
@@ -314,10 +321,6 @@
     for d in order:
         for h in range(2):
             far_send(h, d)
-
-    @pl.loop(0, 2)
-    def _(k):
-        backward([u_start(1 - 2 * k, 1), u_start(1 - 2 * k, -1)])
 
     for h in range(2):
         far_take(h, 2)

time: 62.7 us -> 66.2 us (1.056)
  Pallas kernels: 61.9 us -> 65.1 us
    pallas_call x1, Pallas kernels: 59.9 us -> 63.1 us  [local(): pl.pallas_call(full_kernel, out_shape=(jax.ShapeDtypeStruct((4, 64, 256),...]
where the time goes in v6:
time: 66.2 us; the launch traced here: 65.7 us
  Pallas kernels  65.1 us (98%)
    pallas_call x1, Pallas kernels, local(): pl.pallas_call(full_kernel, out_shape=(jax.ShapeDtypeStruct((4, 64, 256),...  63.1 us
    pallas_call x1, Pallas kernels, settled(): pl.pallas_call(settle_kernel, out_shape=(jax.ShapeDtypeStruct(responses.s...  1.97 us

profile of v6, /device:TPU:32, one launch (start us, length us, event | category | flops | bytes accessed | tf_op | source)
XLA Modules:
  0.0 65.7 jit_solution(736677693205767422)
XLA Ops:
  0.6 63.1 %shard_map.58 = (bf16[4,64,256]{2,1,0:T(8,128)(2,1)}, bf16[8,32,256]{2,1,0:T(8,128)(2,1)}, f32[288,192]{1,0:T(8,128)}) custom-call(bf16[8,32,256]{2,1,0:T(8,128)(2,1)} %vox.1, bf16[27,32,64]{2,1,0:T(8,128)(2,1)} %fl.1, bf16[4,64,256]{2,1,0:T(8,128)(2,1)} %up.1), custom_call_target="tpu_custom_call" | custom-call | tf_op jit(solution)/shard_map/pallas_call | solution.py:413
  63.8 2.0 %shard_map.59 = (bf16[4,64,256]{2,1,0:T(8,128)(2,1)}, bf16[8,32,256]{2,1,0:T(8,128)(2,1)}, f32[27,32,64]{2,1,0:T(8,128)}) custom-call(bf16[4,64,256]{2,1,0:T(8,128)(2,1)} %get-tuple-element.6.r, bf16[8,32,256]{2,1,0:T(8,128)(2,1)} %get-tuple-element.7.v, f32[288,192]{1,0:T(8,128)} %get-tuple-element.8.w), custom_call_target="tpu_custom_call" | custom-call | tf_op jit(solution)/shard_map/pallas_call | solution.py:399
